TPU v7x, 32 devices: a whole 2x2x4 slice. The times are simulated.
32 devices in a mesh: dp: 8 (over y, x, core), tensor: 4 (over z).
Axes of the slice: x: 2, y: 2, z: 4, core: 2. Of those that a mesh axis runs over, the one named last changes fastest.
Arguments:
- block_in: float32 [4096, 1024], P(('dp', 'tensor')), may hold values from -6 to 6
- cotangent: float32 [4096, 1024], P(('dp', 'tensor')), may hold values from -6 to 6
- routes: int32 [4096, 8], P('dp'), may hold values from 0 to 15, all different within a row; in each aligned block of 512 rows (0 to 511, 512 to 1023, ...) at most 288 rows name the same one
- gate_weights: float32 [4096, 8], P('dp'), may hold values from 0.02 to 0.3
- norm_gains: float32 [2, 1024], P(None, 'dp'), may hold values from 0.5 to 1.5
- attention_weight: float32 [4, 1024, 512], P(None, 'dp', 'tensor'), may hold values from -0.1875 to 0.1875
- output_weight: float32 [2, 1024, 512], P(None, 'dp', 'tensor'), may hold values from -0.75 to 0.75
- w_gate_up: float32 [16, 2, 1024, 512], P(None, None, 'dp', 'tensor'), may hold values from -0.1875 to 0.1875
- w_down: float32 [16, 1024, 512], P(None, 'dp', 'tensor'), may hold values from -0.75 to 0.75
- m_gains: float32 [2, 1024], P(None, 'dp'), may hold values from -128 to 128
- v_gains: float32 [2, 1024], P(None, 'dp'), may hold values from 100 to 10000
- attention_first_moment: float32 [4, 1024, 512], P(None, 'dp', 'tensor'), may hold values from -12 to 12
- attention_second_moment: float32 [4, 1024, 512], P(None, 'dp', 'tensor'), may hold values from 1 to 100
- output_first_moment: float32 [2, 1024, 512], P(None, 'dp', 'tensor'), may hold values from -16 to 16
- output_second_moment: float32 [2, 1024, 512], P(None, 'dp', 'tensor'), may hold values from 1 to 100
- m_gate_up: float32 [16, 2, 1024, 512], P(None, None, 'dp', 'tensor'), may hold values from -32 to 32
- v_gate_up: float32 [16, 2, 1024, 512], P(None, None, 'dp', 'tensor'), may hold values from 10 to 1000
- m_down: float32 [16, 1024, 512], P(None, 'dp', 'tensor'), may hold values from -12 to 12
- v_down: float32 [16, 1024, 512], P(None, 'dp', 'tensor'), may hold values from 1 to 100
Outputs:
- block_out: float32 [4096, 1024], P(('dp', 'tensor'))
- input_grad: float32 [4096, 1024], P(('dp', 'tensor'))
- grad_gains: float32 [2, 1024], P(None, 'dp')
- grad_attn: float32 [4, 1024, 512], P(None, 'dp', 'tensor')
- grad_out: float32 [2, 1024, 512], P(None, 'dp', 'tensor')
- grad_gate_up: float32 [16, 2, 1024, 512], P(None, None, 'dp', 'tensor')
- grad_down: float32 [16, 1024, 512], P(None, 'dp', 'tensor')
- new_gains: float32 [2, 1024], P(None, 'dp')
- new_attn: float32 [4, 1024, 512], P(None, 'dp', 'tensor')
- new_out: float32 [2, 1024, 512], P(None, 'dp', 'tensor')
- new_gate_up: float32 [16, 2, 1024, 512], P(None, None, 'dp', 'tensor')
- new_down: float32 [16, 1024, 512], P(None, 'dp', 'tensor')
- new_m_gains: float32 [2, 1024], P(None, 'dp')
- new_v_gains: float32 [2, 1024], P(None, 'dp')
- new_m_attn: float32 [4, 1024, 512], P(None, 'dp', 'tensor')
- new_v_attn: float32 [4, 1024, 512], P(None, 'dp', 'tensor')
- new_m_out: float32 [2, 1024, 512], P(None, 'dp', 'tensor')
- new_v_out: float32 [2, 1024, 512], P(None, 'dp', 'tensor')
- new_m_gate_up: float32 [16, 2, 1024, 512], P(None, None, 'dp', 'tensor')
- new_v_gate_up: float32 [16, 2, 1024, 512], P(None, None, 'dp', 'tensor')
- new_m_down: float32 [16, 1024, 512], P(None, 'dp', 'tensor')
- new_v_down: float32 [16, 1024, 512], P(None, 'dp', 'tensor')
Inputs may be any that keep to these rules, and one draw needn't show every extreme that they name: `routes`: each row names 8 different experts. Within each aligned block of 512 rows no expert is named by more than 288 rows, and in some block one expert is named by exactly 288 rows.
All inputs are finite; a program needn't handle non-finite values.
Results may differ from a plain program's by a relative error of at most 0.015.
The roundings to bfloat16 on the way count: a program that leaves them out, or rounds other values in their place, can miss the bound.
Values may be sent and summed in bfloat16 or wider, within the bound.
A program may use at most 192 MiB of HBM per device.

v0:
```python
import jax
import jax.numpy as jnp
from jax import lax
from jax.sharding import PartitionSpec as P

HEAD_SIZE = 64
SEQ = 512
STEP = 3
norm_eps = 1e-05
beta_one = 0.9
beta_two = 0.95
adam_eps = 1e-08
rate_matrix = 0.02
rate_gain = 0.2
decay_matrix = 0.1
rope_base = 10000.0


def rope_tables(length, width):
    half_width = width // 2
    frequency = rope_base ** (-(2.0 * jnp.arange(half_width, dtype=jnp.float32)) / width)
    angles = jnp.arange(length, dtype=jnp.float32)[:, None] * frequency[None, :]
    return (jnp.cos(angles)[:, None, :], jnp.sin(angles)[:, None, :])


def rotate(vectors, cos_table, sine_table):
    half_width = vectors.shape[-1] // 2
    lower_half = vectors[..., :half_width]
    upper_half = vectors[..., half_width:]
    return jnp.concatenate(
        [
            lower_half * cos_table - upper_half * sine_table,
            upper_half * cos_table + lower_half * sine_table,
        ],
        axis=-1,
    )


def unrotate(vectors, cos_table, sine_table):
    half_width = vectors.shape[-1] // 2
    lower_half = vectors[..., :half_width]
    upper_half = vectors[..., half_width:]
    return jnp.concatenate(
        [
            lower_half * cos_table + upper_half * sine_table,
            upper_half * cos_table - lower_half * sine_table,
        ],
        axis=-1,
    )


def causal_scores(queries, keys_rot):
    scale = queries.shape[-1] ** (-0.5)
    scores = (
        jnp.einsum("jqgh,kgh->jgqk", queries, keys_rot, preferred_element_type=jnp.float32) * scale
    )
    length = scores.shape[-1]
    allowed = lax.broadcasted_iota(jnp.int32, (length, length), 0) >= lax.broadcasted_iota(
        jnp.int32, (length, length), 1
    )
    return jnp.where(allowed, scores, -jnp.inf)


def attend(items):
    queries, keys_rot, values = items
    scores = causal_scores(queries, keys_rot)
    log_totals = jax.nn.logsumexp(scores, axis=-1)
    softmax_b = jnp.exp(scores - log_totals[..., None]).astype(jnp.bfloat16)
    attended = jnp.einsum(
        "jgqk,kgh->jqgh", softmax_b, values, preferred_element_type=jnp.float32
    ).astype(jnp.bfloat16)
    return (attended, log_totals)


def attend_back(items):
    queries, keys_rot, values, attended, log_totals, attended_cot = items
    scale = queries.shape[-1] ** (-0.5)
    scores = causal_scores(queries, keys_rot)
    softmax_f = jnp.exp(scores - log_totals[..., None])
    softmax_b = softmax_f.astype(jnp.bfloat16)
    value_cot = jnp.einsum(
        "jgqk,jqgh->kgh", softmax_b, attended_cot, preferred_element_type=jnp.float32
    )
    weight_cot = jnp.einsum(
        "jqgh,kgh->jgqk", attended_cot, values, preferred_element_type=jnp.float32
    )
    row_dots = jnp.einsum(
        "jqgh,jqgh->jgq", attended_cot, attended, preferred_element_type=jnp.float32
    )
    score_cot = (softmax_f * (weight_cot - row_dots[..., None])).astype(jnp.bfloat16)
    query_cot = (
        jnp.einsum("jgqk,kgh->jqgh", score_cot, keys_rot, preferred_element_type=jnp.float32)
        * scale
    )
    key_cot = (
        jnp.einsum("jgqk,jqgh->kgh", score_cot, queries, preferred_element_type=jnp.float32) * scale
    )
    return (query_cot, key_cot, value_cot)


def adamw_update(weight, moment_one, moment_two, gradient, rate, decay):
    new_one = beta_one * moment_one + (1.0 - beta_one) * gradient
    new_two = beta_two * moment_two + (1.0 - beta_two) * gradient * gradient
    corrected_one = new_one / (1.0 - beta_one**STEP)
    corrected_two = new_two / (1.0 - beta_two**STEP)
    new_weight = weight - rate * (
        corrected_one / (jnp.sqrt(corrected_two) + adam_eps) + decay * weight
    )
    return (new_weight, new_one, new_two)


def local(
    block_in,
    cotangent,
    routes,
    gate_weights,
    norm_gains,
    attention_weight,
    output_weight,
    w_gate_up,
    w_down,
    m_gains,
    v_gains,
    attention_first_moment,
    attention_second_moment,
    output_first_moment,
    output_second_moment,
    m_gate_up,
    v_gate_up,
    m_down,
    v_down,
):
    bf = jnp.bfloat16
    f32 = jnp.float32
    tok_count = routes.shape[0]
    seq_count = tok_count // SEQ
    width = block_in.shape[1]
    experts = w_gate_up.shape[0]
    rows = w_gate_up.shape[2]
    units = w_gate_up.shape[3]
    cols = attention_weight.shape[2]
    kv_count = cols // HEAD_SIZE
    gains_all = lax.all_gather(norm_gains.astype(bf), "dp", axis=1, tiled=True)
    attn_rows = jnp.concatenate([attention_weight, output_weight], axis=0)
    attn_rows = attn_rows.astype(bf).transpose(1, 0, 2).reshape(rows, 6 * cols)
    attn_all = lax.all_gather(attn_rows, "dp", axis=0, tiled=True)
    proj_all = attn_all[:, : 4 * cols]
    out_all = attn_all[:, 4 * cols :]
    gate_up_rows = w_gate_up.astype(bf).transpose(2, 1, 0, 3).reshape(rows, 2 * experts * units)
    down_rows = w_down.astype(bf).transpose(1, 0, 2).reshape(rows, experts * units)
    cos_table, sine_table = rope_tables(SEQ, HEAD_SIZE)
    gain_one = gains_all[0].astype(f32)
    gain_two = gains_all[1].astype(f32)
    inv_one = lax.rsqrt(jnp.mean(block_in * block_in, axis=1, keepdims=True) + norm_eps)
    normed_one = (block_in * inv_one * gain_one).astype(bf)
    tokens_one = lax.all_gather(normed_one, "tensor", axis=0, tiled=True)
    gate_up_all = lax.all_gather(gate_up_rows, "dp", axis=0, tiled=True)
    down_all = lax.all_gather(down_rows, "dp", axis=0, tiled=True)
    cot_all = lax.all_gather(cotangent.astype(bf), "tensor", axis=0, tiled=True)
    projected = jnp.dot(tokens_one, proj_all, preferred_element_type=f32)
    head_vals = projected.reshape(seq_count, SEQ, 4, kv_count, HEAD_SIZE).transpose(2, 0, 1, 3, 4)
    queries = rotate(head_vals[0:2], cos_table, sine_table).astype(bf).transpose(1, 0, 2, 3, 4)
    keys_rot = rotate(head_vals[2], cos_table, sine_table).astype(bf)
    values = head_vals[3].astype(bf)
    attended, log_totals = lax.map(attend, (queries, keys_rot, values))
    attended_flat = attended.transpose(0, 2, 1, 3, 4).reshape(tok_count, 2 * cols)
    partial_value = jnp.dot(attended_flat, out_all.T, preferred_element_type=f32).astype(bf)
    residual = block_in + lax.psum_scatter(
        partial_value, "tensor", scatter_dimension=0, tiled=True
    ).astype(f32)
    inv_two = lax.rsqrt(jnp.mean(residual * residual, axis=1, keepdims=True) + norm_eps)
    normed_two = (residual * inv_two * gain_two).astype(bf)
    tokens_two = lax.all_gather(normed_two, "tensor", axis=0, tiled=True)
    expert_ids = jnp.arange(experts, dtype=jnp.int32)[None, None, :]
    token_weight = jnp.sum(
        jnp.where(routes[:, :, None] == expert_ids, gate_weights[:, :, None], 0.0), axis=1
    )
    weight_wide = jnp.broadcast_to(token_weight[:, :, None], (tok_count, experts, units)).reshape(
        tok_count, experts * units
    )
    half = experts * units
    gate_up = jnp.dot(tokens_two, gate_up_all, preferred_element_type=f32)
    gate_vals = gate_up[:, :half]
    up_vals = gate_up[:, half:]
    sigmoid_vals = jax.nn.sigmoid(gate_vals)
    hidden = (gate_vals * sigmoid_vals * up_vals * weight_wide).astype(bf)
    hidden_cot = jnp.dot(cot_all, down_all, preferred_element_type=f32) * weight_wide
    gate_cot = (
        hidden_cot * up_vals * sigmoid_vals * (1.0 + gate_vals * (1.0 - sigmoid_vals))
    ).astype(bf)
    up_cot = (hidden_cot * gate_vals * sigmoid_vals).astype(bf)
    both_cot = jnp.concatenate([gate_cot, up_cot], axis=1)
    back_sum = lax.dot_general(
        both_cot, gate_up_all, (((1,), (1,)), ((), ())), preferred_element_type=f32
    ).astype(bf)
    normed_two_cot = lax.psum_scatter(back_sum, "tensor", scatter_dimension=0, tiled=True).astype(
        f32
    )
    down_local = lax.dot_general(
        cot_all, hidden, (((0,), (0,)), ((), ())), preferred_element_type=f32
    ).astype(bf)
    gate_up_local = lax.dot_general(
        tokens_two, both_cot, (((0,), (0,)), ((), ())), preferred_element_type=f32
    ).astype(bf)
    mixture = lax.dot_general(
        hidden, down_all, (((1,), (1,)), ((), ())), preferred_element_type=f32
    ).astype(bf)
    block_out = residual + lax.psum_scatter(
        mixture, "tensor", scatter_dimension=0, tiled=True
    ).astype(f32)
    grad_down = lax.psum_scatter(down_local, "dp", scatter_dimension=0, tiled=True)
    grad_down = grad_down.astype(f32).reshape(rows, experts, units).transpose(1, 0, 2)
    grad_gate_up = lax.psum_scatter(gate_up_local, "dp", scatter_dimension=0, tiled=True)
    grad_gate_up = grad_gate_up.astype(f32).reshape(rows, 2, experts, units).transpose(2, 1, 0, 3)
    scaled_two = gain_two * normed_two_cot
    residual_cot = (
        cotangent
        + inv_two * scaled_two
        - residual * inv_two**3 * jnp.mean(scaled_two * residual, axis=1, keepdims=True)
    )
    resid_all = lax.all_gather(residual_cot.astype(bf), "tensor", axis=0, tiled=True)
    out_local = lax.dot_general(
        resid_all, attended_flat, (((0,), (0,)), ((), ())), preferred_element_type=f32
    )
    attended_cot = jnp.dot(resid_all, out_all, preferred_element_type=f32).astype(bf)
    attended_cot = attended_cot.reshape(seq_count, SEQ, 2, kv_count, HEAD_SIZE).transpose(
        0, 2, 1, 3, 4
    )
    query_cot, key_cot, value_cot = lax.map(
        attend_back, (queries, keys_rot, values, attended, log_totals, attended_cot)
    )
    query_plain = unrotate(query_cot, cos_table, sine_table)
    key_plain = unrotate(key_cot, cos_table, sine_table)
    proj_cot = jnp.concatenate(
        [
            query_plain[:, 0].reshape(tok_count, cols),
            query_plain[:, 1].reshape(tok_count, cols),
            key_plain.reshape(tok_count, cols),
            value_cot.reshape(tok_count, cols),
        ],
        axis=1,
    ).astype(bf)
    attn_local = lax.dot_general(
        tokens_one, proj_cot, (((0,), (0,)), ((), ())), preferred_element_type=f32
    )
    norm_terms = lax.dot_general(
        proj_cot, proj_all, (((1,), (1,)), ((), ())), preferred_element_type=f32
    )
    normed_one_cot = lax.psum_scatter(
        norm_terms.astype(bf), "tensor", scatter_dimension=0, tiled=True
    ).astype(f32)
    both_local = jnp.concatenate([attn_local, out_local], axis=1).astype(bf)
    both_sum = lax.psum_scatter(both_local, "dp", scatter_dimension=0, tiled=True).astype(f32)
    both_sum = both_sum.reshape(rows, 6, cols).transpose(1, 0, 2)
    grad_attn = both_sum[:4]
    grad_out = both_sum[4:]
    scaled_one = gain_one * normed_one_cot
    input_grad = (
        residual_cot
        + inv_one * scaled_one
        - block_in * inv_one**3 * jnp.mean(scaled_one * block_in, axis=1, keepdims=True)
    )
    gain_local = jnp.stack(
        [
            jnp.sum(normed_one_cot * block_in * inv_one, axis=0),
            jnp.sum(normed_two_cot * residual * inv_two, axis=0),
        ]
    )
    gain_sum = lax.psum(gain_local, ("dp", "tensor"))
    grad_gains = lax.dynamic_slice_in_dim(gain_sum, lax.axis_index("dp") * rows, rows, axis=1)
    new_gains, new_m_gains, new_v_gains = adamw_update(
        norm_gains, m_gains, v_gains, grad_gains, rate_gain, 0.0
    )
    new_attn, new_m_attn, new_v_attn = adamw_update(
        attention_weight,
        attention_first_moment,
        attention_second_moment,
        grad_attn,
        rate_matrix,
        decay_matrix,
    )
    new_out, new_m_out, new_v_out = adamw_update(
        output_weight,
        output_first_moment,
        output_second_moment,
        grad_out,
        rate_matrix,
        decay_matrix,
    )
    new_gate_up, new_m_gate_up, new_v_gate_up = adamw_update(
        w_gate_up, m_gate_up, v_gate_up, grad_gate_up, rate_matrix, decay_matrix
    )
    new_down, new_m_down, new_v_down = adamw_update(
        w_down, m_down, v_down, grad_down, rate_matrix, decay_matrix
    )
    return (
        block_out,
        input_grad,
        grad_gains,
        grad_attn,
        grad_out,
        grad_gate_up,
        grad_down,
        new_gains,
        new_attn,
        new_out,
        new_gate_up,
        new_down,
        new_m_gains,
        new_v_gains,
        new_m_attn,
        new_v_attn,
        new_m_out,
        new_v_out,
        new_m_gate_up,
        new_v_gate_up,
        new_m_down,
        new_v_down,
    )


def solution(mesh):
    return jax.shard_map(
        local,
        mesh=mesh,
        in_specs=(
            P(("dp", "tensor"), None),
            P(("dp", "tensor"), None),
            P("dp", None),
            P("dp", None),
            P(None, "dp"),
            P(None, "dp", "tensor"),
            P(None, "dp", "tensor"),
            P(None, None, "dp", "tensor"),
            P(None, "dp", "tensor"),
            P(None, "dp"),
            P(None, "dp"),
            P(None, "dp", "tensor"),
            P(None, "dp", "tensor"),
            P(None, "dp", "tensor"),
            P(None, "dp", "tensor"),
            P(None, None, "dp", "tensor"),
            P(None, None, "dp", "tensor"),
            P(None, "dp", "tensor"),
            P(None, "dp", "tensor"),
        ),
        out_specs=(
            P(("dp", "tensor"), None),
            P(("dp", "tensor"), None),
            P(None, "dp"),
            P(None, "dp", "tensor"),
            P(None, "dp", "tensor"),
            P(None, None, "dp", "tensor"),
            P(None, "dp", "tensor"),
            P(None, "dp"),
            P(None, "dp", "tensor"),
            P(None, "dp", "tensor"),
            P(None, None, "dp", "tensor"),
            P(None, "dp", "tensor"),
            P(None, "dp"),
            P(None, "dp"),
            P(None, "dp", "tensor"),
            P(None, "dp", "tensor"),
            P(None, "dp", "tensor"),
            P(None, "dp", "tensor"),
            P(None, None, "dp", "tensor"),
            P(None, None, "dp", "tensor"),
            P(None, "dp", "tensor"),
            P(None, "dp", "tensor"),
        ),
        check_vma=False,
    )
```

profile of v0, /device:TPU:0, one launch (start us, length us, event | category | flops | bytes accessed | tf_op | source)
XLA Modules:
  0.0 598.8 jit_solution(3122732607899009950)
XLA Ops:
  7.9 10.3 %all_gather.24 = bf16[2,1024]{1,0:T(2,128)(2,1)S(1)} all-gather(bf16[2,128]{1,0:T(2,128)(2,1)S(1)} %convert_element_type.108), channel_id=1, replica_groups=mesh['dp'=8,'tensor'=4] {'dp'}, dimensions={1}, use_global_device_ids=true | all-gather | bytes 4608 | tf_op jit(solution)/shard_map/all_gather | solution.py:143
  25.1 25.1 %all-gather.8.cloned.1.call-done = bf16[512,1024]{1,0:T(8,128)(2,1)} async-done(((bf16[128,1024]{1,0:T(8,128)(2,1)}), bf16[512,1024]{1,0:T(8,128)(2,1)}) %all-gather.8.cloned.1.call-update) | async-done | bytes 1048592 | tf_op jit(solution)/shard_map/all_gather | solution.py:156
  50.2 27.6 %all-gather.10.cloned.1.call-done = bf16[1024,768]{0,1:T(8,128)(2,1)} async-done(((bf16[128,768]{0,1:T(8,128)(2,1)}), bf16[1024,768]{0,1:T(8,128)(2,1)}) %all-gather.10.cloned.1.call-update) | async-done | bytes 1572880 | tf_op jit(solution)/shard_map/all_gather | solution.py:146
  77.8 2.3 fusion.21
  84.6 2.5 convolution_convert_fusion.1
  87.2 27.4 %reduce-scatter.12.cloned.1.call-done = bf16[128,1024]{1,0:T(8,128)(2,1)} async-done(((bf16[512,1024]{1,0:T(8,128)(2,1)}), bf16[128,1024]{1,0:T(8,128)(2,1)}) %reduce-scatter.12.cloned.1.call-update) | async-done | bytes 262160 | tf_op jit(solution)/shard_map/reduce_scatter | solution.py:168
  117.6 2.6 copy.89
  122.1 2.3 copy.91
  127.9 16.3 %all-gather.12.cloned.1.call-done = bf16[512,1024]{1,0:T(8,128)(2,1)} async-done(((bf16[128,1024]{1,0:T(8,128)(2,1)}), bf16[512,1024]{1,0:T(8,128)(2,1)}) %all-gather.12.cloned.1.call-update) | async-done | bytes 1048592 | tf_op jit(solution)/shard_map/all_gather | solution.py:173
  144.2 57.6 %all-gather.14.cloned.1.call-done = bf16[1024,4096]{0,1:T(8,128)(2,1)} async-done(((bf16[128,4096]{0,1:T(8,128)(2,1)}), bf16[1024,4096]{0,1:T(8,128)(2,1)}) %all-gather.14.cloned.1.call-update) | async-done | bytes 8388624 | tf_op jit(solution)/shard_map/all_gather | solution.py:157
  201.8 11.5 %fusion.68 = f32[512,4096]{1,0:T(8,128)} fusion(bf16[512,1024]{1,0:T(8,128)(2,1)} %all-gather.12.cloned.1.call-done, bf16[1024,4096]{0,1:T(8,128)(2,1)} %all-gather.14.cloned.1.call-done), kind=kOutput, calls=%fused_computation.141 | convolution fusion | flops 4294967296 | bytes 17825792 | tf_op jit(solution)/shard_map/dot_general | solution.py:182
  213.3 18.5 %all-gather.18.cloned.1.call-done = bf16[512,1024]{1,0:T(8,128)(2,1)} async-done(((bf16[128,1024]{1,0:T(8,128)(2,1)}), bf16[512,1024]{1,0:T(8,128)(2,1)}) %all-gather.18.cloned.1.call-update) | async-done | bytes 1048592 | tf_op jit(solution)/shard_map/all_gather | solution.py:159
  231.8 39.2 %all-gather.16.cloned.1.call-done = bf16[1024,2048]{0,1:T(8,128)(2,1)} async-done(((bf16[128,2048]{0,1:T(8,128)(2,1)}), bf16[1024,2048]{0,1:T(8,128)(2,1)}) %all-gather.16.cloned.1.call-update) | async-done | bytes 4194320 | tf_op jit(solution)/shard_map/all_gather | solution.py:158
  271.0 2.2 broadcast_in_dim.81
  273.2 10.1 %multiply_convert_fusion.1 = (bf16[512,2048]{1,0:T(8,128)(2,1)S(1)}, bf16[512,2048]{1,0:T(8,128)(2,1)S(1)}, bf16[512,2048]{1,0:T(8,128)(2,1)}) fusion(f32[512,4096]{1,0:T(8,128)} %fusion.68, f32[64,8,16,128]{3,2,1,0:T(8,128)S(1)} %bitcast.152, bf16[512,1024]{1,0:T(8,128)(2,1)} %all-gather.18.cloned.1.call-done, ...), kind=kOutput, calls=%fused_computation.11 | convolution fusion | flops 2166358016 | bytes 24117248 | tf_op jit(solution)/shard_map/dot_general | solution.py:187
  285.4 5.5 fusion.9
  291.1 6.1 %convolution_convert_fusion.4 = bf16[512,1024]{1,0:T(8,128)(2,1)} fusion(bf16[512,2048]{1,0:T(8,128)(2,1)} %get-tuple-element.99, bf16[1024,2048]{0,1:T(8,128)(2,1)} %all-gather.16.cloned.1.call-done), kind=kOutput, calls=%fused_computation.32 | convolution fusion | flops 2148007936 | bytes 7340032 | tf_op jit(solution)/shard_map/dot_general | solution.py:205
  297.3 21.0 %reduce-scatter.16.cloned.1.call-done = bf16[128,1024]{1,0:T(8,128)(2,1)} async-done(((bf16[512,1024]{1,0:T(8,128)(2,1)}), bf16[128,1024]{1,0:T(8,128)(2,1)}) %reduce-scatter.16.cloned.1.call-update) | async-done | bytes 262160 | tf_op jit(solution)/shard_map/reduce_scatter | solution.py:196
  320.5 26.5 %reduce-scatter.14.cloned.1.call-done = bf16[128,1024]{1,0:T(8,128)(2,1)} async-done(((bf16[512,1024]{1,0:T(8,128)(2,1)}), bf16[128,1024]{1,0:T(8,128)(2,1)}) %reduce-scatter.14.cloned.1.call-update) | async-done | bytes 262160 | tf_op jit(solution)/shard_map/reduce_scatter | solution.py:208
  347.0 2.5 fusion.65
  349.6 26.6 %all-gather.20.cloned.1.call-done = bf16[512,1024]{1,0:T(8,128)(2,1)} async-done(((bf16[128,1024]{1,0:T(8,128)(2,1)}), bf16[512,1024]{1,0:T(8,128)(2,1)}) %all-gather.20.cloned.1.call-update) | async-done | bytes 1048592 | tf_op jit(solution)/shard_map/all_gather | solution.py:221
  379.1 3.8 fusion.2
  387.8 2.0 convolution_convert_fusion.2
  391.6 6.1 %convert_bitcast_fusion = bf16[1024,2048]{0,1:T(8,128)(2,1)} fusion(bf16[512,2048]{1,0:T(8,128)(2,1)} %get-tuple-element.99, bf16[512,1024]{1,0:T(8,128)(2,1)S(1)} %copy-done.37), kind=kOutput, calls=%fused_computation.9 | convolution fusion | flops 2149580800 | bytes 7340032 | tf_op jit(solution)/shard_map/dot_general | solution.py:199
  397.7 6.5 %copy.115 = bf16[1024,2048]{1,0:T(8,128)(2,1)} copy(bf16[1024,2048]{0,1:T(8,128)(2,1)} %convert_bitcast_fusion) | data formatting | bytes 8388608
  405.5 9.0 %convolution_convert_fusion = bf16[1024,4096]{1,0:T(8,128)(2,1)} fusion(bf16[512,1024]{1,0:T(8,128)(2,1)S(1)} %copy-done.36, bf16[512,2048]{1,0:T(8,128)(2,1)} %copy-done.40, bf16[512,2048]{1,0:T(8,128)(2,1)} %copy-done.39), kind=kOutput, calls=%fused_computation | convolution fusion | flops 4307550208 | bytes 13631488 | tf_op jit(solution)/shard_map/dot_general | solution.py:202
  416.3 40.0 %psum.7 = f32[2,1024]{1,0:T(2,128)S(1)} all-reduce(f32[2,1024]{1,0:T(2,128)S(1)} %pad_maximum_fusion.14), channel_id=1, replica_groups=mesh['dp'=8,'tensor'=4] {'dp','tensor'}, use_global_device_ids=true, to_apply=%region_13.14 | all-reduce | flops 2048 | bytes 16384 | tf_op jit(solution)/shard_map/psum | solution.py:269
  457.0 1.9 fusion.28
  462.0 47.7 %reduce-scatter.24.cloned.1.call-done = bf16[128,2048]{1,0:T(8,128)(2,1)} async-done(((bf16[1024,2048]{1,0:T(8,128)(2,1)}), bf16[128,2048]{1,0:T(8,128)(2,1)}) %reduce-scatter.24.cloned.1.call-update) | async-done | bytes 524304
  512.3 3.7 multiply_subtract_fusion.1
  516.0 68.6 %reduce-scatter.20.cloned.1.call-done = bf16[128,4096]{1,0:T(8,128)(2,1)} async-done(((bf16[1024,4096]{1,0:T(8,128)(2,1)}), bf16[128,4096]{1,0:T(8,128)(2,1)}) %reduce-scatter.20.cloned.1.call-update) | async-done | bytes 1048592 | tf_op jit(solution)/shard_map/reduce_scatter | solution.py:213
  587.1 4.9 multiply_subtract_fusion
  (173 shorter events, 46.0 us)
Async XLA Ops:
  7.2 43.0 %all-gather.8.cloned.1.call-start = ((), (), s32[]{:S(2)}) async-start(), calls=%async_computation.7 | async-start | bytes 1310720 | tf_op jit(solution)/shard_map/all_gather | solution.py:156
  21.8 56.1 %all-gather.10.cloned.1.call-start = ((), (), s32[]{:S(2)}) async-start(), calls=%async_computation.8 | async-start | bytes 1769472 | tf_op jit(solution)/shard_map/all_gather | solution.py:146
  24.6 89.9 %reduce-scatter.12.cloned.1.call-start = ((), (), s32[]{:S(2)}) async-start(), calls=%async_computation.9 | async-start | bytes 1310720 | tf_op jit(solution)/shard_map/reduce_scatter | solution.py:168
  24.8 58.2 %copy-start.7 = (pred[512,512]{0,1:T(8,128)(4,1)}, pred[512,512]{0,1:T(8,128)(4,1)S(1)}, u32[]{:S(2)}) copy-start(pred[512,512]{0,1:T(8,128)(4,1)S(1)} %iota_compare_fusion) | copy-start | bytes 786436
  84.0 30.5 %copy-start.1 = (f32[128,1024]{1,0:T(8,128)S(1)}, f32[128,1024]{1,0:T(8,128)}, u32[]{:S(2)}) copy-start(f32[128,1024]{1,0:T(8,128)} %param.19) | copy-start | bytes 1572868
  87.1 57.1 %all-gather.12.cloned.1.call-start = ((), (), s32[]{:S(2)}) async-start(), calls=%async_computation.10 | async-start | bytes 1310720 | tf_op jit(solution)/shard_map/all_gather | solution.py:173
  117.6 84.2 %all-gather.14.cloned.1.call-start = ((), (), s32[]{:S(2)}) async-start(), calls=%async_computation.11 | async-start | bytes 9437184 | tf_op jit(solution)/shard_map/all_gather | solution.py:157
  120.2 111.6 %all-gather.18.cloned.1.call-start = ((), (), s32[]{:S(2)}) async-start(), calls=%async_computation.14 | async-start | bytes 1310720 | tf_op jit(solution)/shard_map/all_gather | solution.py:159
  122.0 148.9 %all-gather.16.cloned.1.call-start = ((), (), s32[]{:S(2)}) async-start(), calls=%async_computation.12 | async-start | bytes 4718592 | tf_op jit(solution)/shard_map/all_gather | solution.py:158
  124.4 193.9 %reduce-scatter.16.cloned.1.call-start = ((), (), s32[]{:S(2)}) async-start(), calls=%async_computation.15 | async-start | bytes 1310720 | tf_op jit(solution)/shard_map/reduce_scatter | solution.py:196
  271.0 14.4 %slice-start = ((s8[8388608]{0:T(1024)(128)(4,1)}), s8[4194304]{0:T(1024)(128)(4,1)S(1)}, s32[]{:S(2)}) async-start(s8[8388608]{0:T(1024)(128)(4,1)} %bitcast.179), calls=%async_computation.21 | async-start | bytes 8388608
  273.2 12.1 %slice-start.1 = ((s8[8388608]{0:T(1024)(128)(4,1)}), s8[4194304]{0:T(1024)(128)(4,1)S(1)}, s32[]{:S(2)}) async-start(s8[8388608]{0:T(1024)(128)(4,1)} %bitcast.179), calls=%async_computation.22 | async-start | bytes 8388608
  290.8 56.2 %reduce-scatter.14.cloned.1.call-start = ((), (), s32[]{:S(2)}) async-start(), calls=%async_computation.13 | async-start | bytes 1310720 | tf_op jit(solution)/shard_map/reduce_scatter | solution.py:208
  297.2 78.9 %all-gather.20.cloned.1.call-start = ((), (), s32[]{:S(2)}) async-start(), calls=%async_computation.16 | async-start | bytes 1310720 | tf_op jit(solution)/shard_map/all_gather | solution.py:221
  349.5 29.5 %copy-start.8 = (pred[512,512]{0,1:T(8,128)(4,1)S(1)}, pred[512,512]{0,1:T(8,128)(4,1)}, u32[]{:S(2)}) copy-start(pred[512,512]{0,1:T(8,128)(4,1)} %copy-done.7) | copy-start | bytes 786436
  349.5 65.2 %reduce-scatter.18.cloned.1.call-start = ((), (), s32[]{:S(2)}) async-start(), calls=%async_computation.17 | async-start | bytes 1310720 | tf_op jit(solution)/shard_map/reduce_scatter | solution.py:249
  387.3 71.6 %reduce-scatter.22.cloned.1.call-start = ((), (), s32[]{:S(2)}) async-start(), calls=%async_computation.19 | async-start | bytes 1769472
  391.5 118.2 %reduce-scatter.24.cloned.1.call-start = ((), (), s32[]{:S(2)}) async-start(), calls=%async_computation.20 | async-start | bytes 4718592
  404.3 180.4 %reduce-scatter.20.cloned.1.call-start = ((), (), s32[]{:S(2)}) async-start(), calls=%async_computation.18 | async-start | bytes 9437184 | tf_op jit(solution)/shard_map/reduce_scatter | solution.py:213
  414.5 41.9 %copy-start.32 = (f32[2,128]{1,0:T(2,128)S(1)}, f32[2,128]{1,0:T(2,128)}, u32[]{:S(2)}) copy-start(f32[2,128]{1,0:T(2,128)} %param.23) | copy-start | bytes 3076
  414.5 41.9 %copy-start.33 = (f32[2,128]{1,0:T(2,128)S(1)}, f32[2,128]{1,0:T(2,128)}, u32[]{:S(2)}) copy-start(f32[2,128]{1,0:T(2,128)} %param.28) | copy-start | bytes 3076
  414.5 41.8 %copy-start.34 = (f32[2,128]{1,0:T(2,128)S(1)}, f32[2,128]{1,0:T(2,128)}, u32[]{:S(2)}) copy-start(f32[2,128]{1,0:T(2,128)} %param.29) | copy-start | bytes 3076
  414.5 42.4 %copy-start.10 = (f32[128,1024]{1,0:T(8,128)S(1)}, f32[128,1024]{1,0:T(8,128)}, u32[]{:S(2)}) copy-start(f32[128,1024]{1,0:T(8,128)} %get-tuple-element.94) | copy-start | bytes 1572868
  414.5 42.4 %copy-start.35 = (f32[128]{0:T(128)S(1)}, f32[128]{0:T(128)}, u32[]{:S(2)}) copy-start(f32[128]{0:T(128)} %get-tuple-element.113) | copy-start | bytes 1540
  414.6 45.6 %copy-start.19 = (f32[2,128,128]{2,1,0:T(8,128)S(1)}, f32[2,128,128]{2,1,0:T(8,128)}, u32[]{:S(2)}) copy-start(f32[2,128,128]{2,1,0:T(8,128)} %param.25) | copy-start | bytes 393220
  414.6 45.6 %copy-start.26 = (f32[2,128,128]{2,1,0:T(8,128)S(1)}, f32[2,128,128]{2,1,0:T(8,128)}, u32[]{:S(2)}) copy-start(f32[2,128,128]{2,1,0:T(8,128)} %param.32) | copy-start | bytes 393220
  414.6 45.6 %copy-start.27 = (f32[2,128,128]{2,1,0:T(8,128)S(1)}, f32[2,128,128]{2,1,0:T(8,128)}, u32[]{:S(2)}) copy-start(f32[2,128,128]{2,1,0:T(8,128)} %param.33) | copy-start | bytes 393220
  414.6 46.4 %copy-start.13 = (f32[4,128,128]{2,1,0:T(8,128)S(1)}, f32[4,128,128]{2,1,0:T(8,128)}, u32[]{:S(2)}) copy-start(f32[4,128,128]{2,1,0:T(8,128)} %param.24) | copy-start | bytes 786436
  414.6 46.4 %copy-start.24 = (f32[4,128,128]{2,1,0:T(8,128)S(1)}, f32[4,128,128]{2,1,0:T(8,128)}, u32[]{:S(2)}) copy-start(f32[4,128,128]{2,1,0:T(8,128)} %param.30) | copy-start | bytes 786436
  414.6 46.4 %copy-start.25 = (f32[4,128,128]{2,1,0:T(8,128)S(1)}, f32[4,128,128]{2,1,0:T(8,128)}, u32[]{:S(2)}) copy-start(f32[4,128,128]{2,1,0:T(8,128)} %param.31) | copy-start | bytes 786436
  460.0 52.3 %copy-start.3 = (f32[16,128,128]{2,1,0:T(8,128)S(1)}, f32[16,128,128]{2,1,0:T(8,128)}, u32[]{:S(2)}) copy-start(f32[16,128,128]{2,1,0:T(8,128)} %param.27) | copy-start | bytes 3145732
  516.0 70.5 %copy-start.2 = (f32[16,2,128,128]{3,2,1,0:T(8,128)S(1)}, f32[16,2,128,128]{3,2,1,0:T(8,128)}, u32[]{:S(2)}) copy-start(f32[16,2,128,128]{3,2,1,0:T(8,128)} %param.26) | copy-start | bytes 6291460
  (25 other events, 51.2 us)
Sparse Core Ops, SparseCore 0:
  21.9 28.2 all-gather.7
  52.6 25.1 all-gather.9
  87.3 27.2 reduce-scatter.11
  117.7 26.4 all-gather.11
  146.5 55.2 all-gather.13
  203.8 27.9 all-gather.17
  234.2 36.7 all-gather.15
  291.0 27.2 reduce-scatter.15
  321.2 25.7 reduce-scatter.13
  349.6 26.4 all-gather.19
  387.4 26.6 reduce-scatter.17
  417.8 37.1 reduce-scatter.21
  458.3 51.3 reduce-scatter.23
  513.1 71.4 reduce-scatter.19
where the time goes:
time: 605 us; the launch traced here: 599 us
  waiting for transfers between devices  402 us (66%)
  matrix products  66.3 us (11%)
  blocking collectives  50.3 us (8%)
  other arithmetic  34.6 us (6%)
  local copies, waits for them, and re-layouts  29 us (5%)
  between operations  14.9 us (2%)
    reduce_scatter x1, waiting for transfers between devices, local(): lax.psum_scatter(gate_up_local, 'dp', scatter_dimension=0, tiled=True)  68.6 us
    all_gather x1, waiting for transfers between devices, local(): gate_up_all = lax.all_gather(gate_up_rows, 'dp', axis=0, tiled=True)  57.6 us
    unnamed x16, waiting for transfers between devices  48 us
    psum x1, blocking collectives, local(): gain_sum = lax.psum(gain_local, ('dp', 'tensor'))  40 us
    all_gather x1, waiting for transfers between devices, local(): down_all = lax.all_gather(down_rows, 'dp', axis=0, tiled=True)  39.2 us
    all_gather x1, waiting for transfers between devices, local(): attn_all = lax.all_gather(attn_rows, 'dp', axis=0, tiled=True)  27.6 us
    reduce_scatter x1, waiting for transfers between devices, local(): lax.psum_scatter(partial_value, 'tensor', scatter_dimension=0, tiled=True)  27.4 us
    all_gather x1, waiting for transfers between devices, local(): lax.all_gather(residual_cot.astype(bf), 'tensor', axis=0, tiled=True)  26.6 us
  transfers between devices with their start and end apart: 14, of which 12 were waited for; matrix products, arithmetic and copies ran while one was open for 12% of the time, Pallas kernels for 0%

commit v1 on v0

--- a/solution.py
+++ b/solution.py
@@ -14,6 +14,22 @@
 rate_gain = 0.2
 decay_matrix = 0.1
 rope_base = 10000.0
+
+
+def collect(x, axis, dim):
+    ways, here, step = (lax.axis_size(axis), lax.axis_index(axis), x.shape[dim])
+    shape = [n * ways if d == dim else n for d, n in enumerate(x.shape)]
+    full = lax.dynamic_update_slice_in_dim(jnp.zeros(shape, x.dtype), x, here * step, axis=dim)
+    going_up = going_down = x
+    for far in range(1, ways // 2 + 1):
+        going_up = lax.ppermute(going_up, axis, [(d, (d + 1) % ways) for d in range(ways)])
+        full = lax.dynamic_update_slice_in_dim(full, going_up, (here - far) % ways * step, axis=dim)
+        if 2 * far < ways:
+            going_down = lax.ppermute(going_down, axis, [(d, (d - 1) % ways) for d in range(ways)])
+            full = lax.dynamic_update_slice_in_dim(
+                full, going_down, (here + far) % ways * step, axis=dim
+            )
+    return full
 
 
 def rope_tables(length, width):
@@ -155,7 +171,7 @@
     normed_one = (block_in * inv_one * gain_one).astype(bf)
     tokens_one = lax.all_gather(normed_one, "tensor", axis=0, tiled=True)
     gate_up_all = lax.all_gather(gate_up_rows, "dp", axis=0, tiled=True)
-    down_all = lax.all_gather(down_rows, "dp", axis=0, tiled=True)
+    down_all = collect(down_rows, "dp", 0)
     cot_all = lax.all_gather(cotangent.astype(bf), "tensor", axis=0, tiled=True)
     projected = jnp.dot(tokens_one, proj_all, preferred_element_type=f32)
     head_vals = projected.reshape(seq_count, SEQ, 4, kv_count, HEAD_SIZE).transpose(2, 0, 1, 3, 4)

time: 605 us -> 573 us (0.947)
  waiting for transfers between devices: 402 us -> 349 us
  local copies, waits for them, and re-layouts: 29 us -> 41.4 us
  starting transfers between devices: 1.43 us -> 9.48 us
    all_gather x1 -> x0, waiting for transfers between devices: 39.2 us -> none  [local(): down_all = lax.all_gather(down_rows, 'dp', axis=0, tiled=True)]
    ppermute x0 -> x7, waiting for transfers between devices: none -> 32 us  [the longest x3 19.9 us: collect(): lax.ppermute(going_down, axis, [(d, (d - 1) % ways) for d in range(ways)])]
    all_gather x1, waiting for transfers between devices: 57.6 us -> 28 us  [local(): gate_up_all = lax.all_gather(gate_up_rows, 'dp', axis=0, tiled=True)]
    all_gather x1, waiting for transfers between devices: 16.3 us -> 0.01 us  [local(): tokens_two = lax.all_gather(normed_two, 'tensor', axis=0, tiled=True)]
    dynamic_update_slice x0 -> x8, local copies, waits for them, and re-layouts: none -> 11.3 us  [the longest x4 5.68 us: collect(): lax.dynamic_update_slice_in_dim(full, going_up, (here - far) % ways * ste...]
    ppermute x0 -> x7, starting transfers between devices: none -> 8.56 us  [the longest x3 8.1 us: collect(): lax.ppermute(going_down, axis, [(d, (d - 1) % ways) for d in range(ways)])]
    unnamed x95 -> x103, local copies, waits for them, and re-layouts: 24.7 us -> 23.2 us
    unnamed x16 -> x15, waiting for transfers between devices: 48 us -> 47.8 us
  transfers between devices with their start and end apart: 14 -> 20, of which waited for: 12 -> 14; matrix products, arithmetic and copies ran while one was open for 12% -> 15% of each run, Pallas kernels for 0% -> 0%
where the time goes in v1:
time: 573 us; the launch traced here: 566 us
  waiting for transfers between devices  349 us (61%)
  matrix products  66.5 us (12%)
  blocking collectives  50.3 us (9%)
  local copies, waits for them, and re-layouts  41.4 us (7%)
  other arithmetic  34.5 us (6%)
  between operations  14.9 us (3%)
  starting transfers between devices  9.48 us (2%)
    reduce_scatter x1, waiting for transfers between devices, local(): lax.psum_scatter(gate_up_local, 'dp', scatter_dimension=0, tiled=True)  69.3 us
    unnamed x15, waiting for transfers between devices  47.8 us
    psum x1, blocking collectives, local(): gain_sum = lax.psum(gain_local, ('dp', 'tensor'))  40 us
    all_gather x1, waiting for transfers between devices, local(): gate_up_all = lax.all_gather(gate_up_rows, 'dp', axis=0, tiled=True)  28 us
    all_gather x1, waiting for transfers between devices, local(): attn_all = lax.all_gather(attn_rows, 'dp', axis=0, tiled=True)  27.6 us
    reduce_scatter x1, waiting for transfers between devices, local(): lax.psum_scatter(partial_value, 'tensor', scatter_dimension=0, tiled=True)  27.4 us
    all_gather x1, waiting for transfers between devices, local(): lax.all_gather(residual_cot.astype(bf), 'tensor', axis=0, tiled=True)  26.6 us
    reduce_scatter x1, waiting for transfers between devices, local(): lax.psum_scatter(mixture, 'tensor', scatter_dimension=0, tiled=True)  26.4 us
  transfers between devices with their start and end apart: 20, of which 14 were waited for; matrix products, arithmetic and copies ran while one was open for 15% of the time, Pallas kernels for 0%

profile of v1, /device:TPU:0, one launch (start us, length us, event | category | flops | bytes accessed | tf_op | source)
XLA Modules:
  0.0 566.1 jit_solution(13602315837350771751)
XLA Ops:
  9.7 10.3 %all_gather.21 = bf16[2,1024]{1,0:T(2,128)(2,1)S(1)} all-gather(bf16[2,128]{1,0:T(2,128)(2,1)S(1)} %convert_element_type.108), channel_id=1, replica_groups=mesh['dp'=8,'tensor'=4] {'dp'}, dimensions={1}, use_global_device_ids=true | all-gather | bytes 4608 | tf_op jit(solution)/shard_map/all_gather | solution.py:159
  25.2 25.1 %all-gather.7.cloned.1.call-done = bf16[512,1024]{1,0:T(8,128)(2,1)} async-done(((bf16[128,1024]{1,0:T(8,128)(2,1)}), bf16[512,1024]{1,0:T(8,128)(2,1)}) %all-gather.7.cloned.1.call-update) | async-done | bytes 1048592 | tf_op jit(solution)/shard_map/all_gather | solution.py:172
  50.3 27.6 %all-gather.9.cloned.1.call-done = bf16[1024,768]{0,1:T(8,128)(2,1)} async-done(((bf16[128,768]{0,1:T(8,128)(2,1)}), bf16[1024,768]{0,1:T(8,128)(2,1)}) %all-gather.9.cloned.1.call-update) | async-done | bytes 1572880 | tf_op jit(solution)/shard_map/all_gather | solution.py:162
  83.9 2.5 convolution_convert_fusion.1
  86.5 27.4 %reduce-scatter.12.cloned.1.call-done = bf16[128,1024]{1,0:T(8,128)(2,1)} async-done(((bf16[512,1024]{1,0:T(8,128)(2,1)}), bf16[128,1024]{1,0:T(8,128)(2,1)}) %reduce-scatter.12.cloned.1.call-update) | async-done | bytes 262160 | tf_op jit(solution)/shard_map/reduce_scatter | solution.py:184
  116.9 2.6 copy.92
  121.8 2.6 collective-permute-start.1
  124.4 11.0 %collective-permute-done = bf16[128,2048]{0,1:T(8,128)(2,1)} collective-permute-done((bf16[128,2048]{0,1:T(8,128)(2,1)}, bf16[128,2048]{0,1:T(8,128)(2,1)}, u32[]{:S(2)}, u32[]{:S(2)}) %collective-permute-start) | collective-permute-done | bytes 524320 | tf_op jit(solution)/shard_map/ppermute | solution.py:25
  137.3 2.6 broadcast_in_dim.85
  140.8 2.7 collective-permute-start.3
  149.6 6.3 %collective-permute-done.3 = bf16[128,2048]{0,1:T(8,128)(2,1)} collective-permute-done((bf16[128,2048]{0,1:T(8,128)(2,1)}, bf16[128,2048]{0,1:T(8,128)(2,1)}, u32[]{:S(2)}, u32[]{:S(2)}) %collective-permute-start.3) | collective-permute-done | bytes 524320 | tf_op jit(solution)/shard_map/ppermute | solution.py:28
  155.9 2.8 collective-permute-start.5
  163.9 13.6 %collective-permute-done.5 = bf16[128,2048]{0,1:T(8,128)(2,1)S(1)} collective-permute-done((bf16[128,2048]{0,1:T(8,128)(2,1)}, bf16[128,2048]{0,1:T(8,128)(2,1)S(1)}, u32[]{:S(2)}, u32[]{:S(2)}) %collective-permute-start.5) | collective-permute-done | bytes 524320 | tf_op jit(solution)/shard_map/ppermute | solution.py:28
  180.4 28.0 %all-gather.13.cloned.1.call-done = bf16[1024,4096]{0,1:T(8,128)(2,1)} async-done(((bf16[128,4096]{0,1:T(8,128)(2,1)}), bf16[1024,4096]{0,1:T(8,128)(2,1)}) %all-gather.13.cloned.1.call-update) | async-done | bytes 8388624 | tf_op jit(solution)/shard_map/all_gather | solution.py:173
  208.4 11.6 %fusion.68 = f32[512,4096]{1,0:T(8,128)} fusion(bf16[512,1024]{1,0:T(8,128)(2,1)} %all-gather.11.cloned.1.call-done, bf16[1024,4096]{0,1:T(8,128)(2,1)} %all-gather.13.cloned.1.call-done), kind=kOutput, calls=%fused_computation.149 | convolution fusion | flops 4294967296 | bytes 17825792 | tf_op jit(solution)/shard_map/dot_general | solution.py:198
  220.0 18.4 %all-gather.15.cloned.1.call-done = bf16[512,1024]{1,0:T(8,128)(2,1)} async-done(((bf16[128,1024]{1,0:T(8,128)(2,1)}), bf16[512,1024]{1,0:T(8,128)(2,1)}) %all-gather.15.cloned.1.call-update) | async-done | bytes 1048592 | tf_op jit(solution)/shard_map/all_gather | solution.py:175
  240.7 11.3 %multiply_convert_fusion.1 = (bf16[512,2048]{1,0:T(8,128)(2,1)S(1)}, bf16[512,2048]{1,0:T(8,128)(2,1)S(1)}, bf16[512,2048]{1,0:T(8,128)(2,1)}) fusion(f32[512,4096]{1,0:T(8,128)} %fusion.68, f32[64,8,16,128]{3,2,1,0:T(8,128)S(1)} %bitcast.154, bf16[1024,2048]{0,1:T(8,128)(2,1)} %constant_dynamic-update-slice_fusion, ...), kind=kOutput, calls=%fused_computation.11 | convolution fusion | flops 2166358016 | bytes 24117248 | tf_op jit(solution)/shard_map/dot_general | solution.py:203
  254.0 5.5 fusion.9
  259.7 6.1 %convolution_convert_fusion.4 = bf16[512,1024]{1,0:T(8,128)(2,1)} fusion(bf16[512,2048]{1,0:T(8,128)(2,1)} %get-tuple-element.99, bf16[1024,2048]{0,1:T(8,128)(2,1)} %constant_dynamic-update-slice_fusion), kind=kOutput, calls=%fused_computation.32 | convolution fusion | flops 2148007936 | bytes 7340032 | tf_op jit(solution)/shard_map/dot_general | solution.py:221
  265.9 20.4 %reduce-scatter.16.cloned.1.call-done = bf16[128,1024]{1,0:T(8,128)(2,1)} async-done(((bf16[512,1024]{1,0:T(8,128)(2,1)}), bf16[128,1024]{1,0:T(8,128)(2,1)}) %reduce-scatter.16.cloned.1.call-update) | async-done | bytes 262160 | tf_op jit(solution)/shard_map/reduce_scatter | solution.py:212
  288.6 26.4 %reduce-scatter.14.cloned.1.call-done = bf16[128,1024]{1,0:T(8,128)(2,1)} async-done(((bf16[512,1024]{1,0:T(8,128)(2,1)}), bf16[128,1024]{1,0:T(8,128)(2,1)}) %reduce-scatter.14.cloned.1.call-update) | async-done | bytes 262160 | tf_op jit(solution)/shard_map/reduce_scatter | solution.py:224
  315.0 2.5 fusion.65
  317.6 26.6 %all-gather.17.cloned.1.call-done = bf16[512,1024]{1,0:T(8,128)(2,1)} async-done(((bf16[128,1024]{1,0:T(8,128)(2,1)}), bf16[512,1024]{1,0:T(8,128)(2,1)}) %all-gather.17.cloned.1.call-update) | async-done | bytes 1048592 | tf_op jit(solution)/shard_map/all_gather | solution.py:237
  348.0 2.6 fusion.2
  358.2 6.1 %convert_bitcast_fusion = bf16[1024,2048]{0,1:T(8,128)(2,1)} fusion(bf16[512,2048]{1,0:T(8,128)(2,1)} %get-tuple-element.99, bf16[512,1024]{1,0:T(8,128)(2,1)S(1)} %copy-done.41), kind=kOutput, calls=%fused_computation.9 | convolution fusion | flops 2149580800 | bytes 7340032 | tf_op jit(solution)/shard_map/dot_general | solution.py:215
  364.3 6.5 %copy.120 = bf16[1024,2048]{1,0:T(8,128)(2,1)} copy(bf16[1024,2048]{0,1:T(8,128)(2,1)} %convert_bitcast_fusion) | data formatting | bytes 8388608
  372.1 9.0 %convolution_convert_fusion = bf16[1024,4096]{1,0:T(8,128)(2,1)} fusion(bf16[512,1024]{1,0:T(8,128)(2,1)S(1)} %copy-done.40, bf16[512,2048]{1,0:T(8,128)(2,1)} %copy-done.44, bf16[512,2048]{1,0:T(8,128)(2,1)} %copy-done.43), kind=kOutput, calls=%fused_computation | convolution fusion | flops 4307550208 | bytes 13631488 | tf_op jit(solution)/shard_map/dot_general | solution.py:218
  382.9 40.0 %psum.7 = f32[2,1024]{1,0:T(2,128)S(1)} all-reduce(f32[2,1024]{1,0:T(2,128)S(1)} %pad_maximum_fusion.14), channel_id=1, replica_groups=mesh['dp'=8,'tensor'=4] {'dp','tensor'}, use_global_device_ids=true, to_apply=%region_13.14 | all-reduce | flops 2048 | bytes 16384 | tf_op jit(solution)/shard_map/psum | solution.py:285
  428.7 47.5 %reduce-scatter.24.cloned.1.call-done = bf16[128,2048]{1,0:T(8,128)(2,1)} async-done(((bf16[1024,2048]{1,0:T(8,128)(2,1)}), bf16[128,2048]{1,0:T(8,128)(2,1)}) %reduce-scatter.24.cloned.1.call-update) | async-done | bytes 524304
  477.8 4.2 multiply_subtract_fusion.1
  482.0 69.3 %reduce-scatter.20.cloned.1.call-done = bf16[128,4096]{1,0:T(8,128)(2,1)} async-done(((bf16[1024,4096]{1,0:T(8,128)(2,1)}), bf16[128,4096]{1,0:T(8,128)(2,1)}) %reduce-scatter.20.cloned.1.call-update) | async-done | bytes 1048592 | tf_op jit(solution)/shard_map/reduce_scatter | solution.py:229
  554.4 4.9 multiply_subtract_fusion
  (201 shorter events, 67.1 us)
Async XLA Ops:
  7.2 43.1 %all-gather.7.cloned.1.call-start = ((), (), s32[]{:S(2)}) async-start(), calls=%async_computation.7 | async-start | bytes 1310720 | tf_op jit(solution)/shard_map/all_gather | solution.py:172
  21.8 56.1 %all-gather.9.cloned.1.call-start = ((), (), s32[]{:S(2)}) async-start(), calls=%async_computation.8 | async-start | bytes 1769472 | tf_op jit(solution)/shard_map/all_gather | solution.py:162
  24.7 89.2 %reduce-scatter.12.cloned.1.call-start = ((), (), s32[]{:S(2)}) async-start(), calls=%async_computation.9 | async-start | bytes 1310720 | tf_op jit(solution)/shard_map/reduce_scatter | solution.py:184
  24.9 57.5 %copy-start.8 = (pred[512,512]{0,1:T(8,128)(4,1)}, pred[512,512]{0,1:T(8,128)(4,1)S(1)}, u32[]{:S(2)}) copy-start(pred[512,512]{0,1:T(8,128)(4,1)S(1)} %iota_compare_fusion) | copy-start | bytes 786436
  86.5 94.0 %all-gather.11.cloned.1.call-start = ((), (), s32[]{:S(2)}) async-start(), calls=%async_computation.10 | async-start | bytes 1310720 | tf_op jit(solution)/shard_map/all_gather | solution.py:189
  116.9 91.5 %all-gather.13.cloned.1.call-start = ((), (), s32[]{:S(2)}) async-start(), calls=%async_computation.11 | async-start | bytes 9437184 | tf_op jit(solution)/shard_map/all_gather | solution.py:173
  119.5 118.9 %all-gather.15.cloned.1.call-start = ((), (), s32[]{:S(2)}) async-start(), calls=%async_computation.13 | async-start | bytes 1310720 | tf_op jit(solution)/shard_map/all_gather | solution.py:175
  121.8 13.7 %collective-permute-start = (bf16[128,2048]{0,1:T(8,128)(2,1)}, bf16[128,2048]{0,1:T(8,128)(2,1)}, u32[]{:S(2)}, u32[]{:S(2)}) collective-permute-start(bf16[128,2048]{0,1:T(8,128)(2,1)} %bitcast.159), channel_id=1, source_target_pairs={{0,4},{4,8},{8,12},{12,16},{16,20},{20,24},{24,28},{28,0},{1,5},{5... | collective-permute-start | bytes 1572872 | tf_op jit(solution)/shard_map/ppermute | solution.py:25
  121.8 19.0 %collective-permute-start.1 = (bf16[128,2048]{0,1:T(8,128)(2,1)}, bf16[128,2048]{0,1:T(8,128)(2,1)}, u32[]{:S(2)}, u32[]{:S(2)}) collective-permute-start(bf16[128,2048]{0,1:T(8,128)(2,1)} %bitcast.160), channel_id=1, source_target_pairs={{0,28},{4,0},{8,4},{12,8},{16,12},{20,16},{24,20},{28,24},{1,29},{... | collective-permute-start | bytes 1572872 | tf_op jit(solution)/shard_map/ppermute | solution.py:28
  135.4 10.3 %collective-permute-start.2 = (bf16[128,2048]{0,1:T(8,128)(2,1)}, bf16[128,2048]{0,1:T(8,128)(2,1)}, u32[]{:S(2)}, u32[]{:S(2)}) collective-permute-start(bf16[128,2048]{0,1:T(8,128)(2,1)} %collective-permute-done), channel_id=1, source_target_pairs={{0,4},{4,8},{8,12},{12,16},{16,20},{20,24},{24,28},{28,0},{1,5},{5... | collective-permute-start | bytes 1572872 | tf_op jit(solution)/shard_map/ppermute | solution.py:25
  137.3 149.1 %reduce-scatter.16.cloned.1.call-start = ((), (), s32[]{:S(2)}) async-start(), calls=%async_computation.14 | async-start | bytes 1310720 | tf_op jit(solution)/shard_map/reduce_scatter | solution.py:212
  140.8 15.1 %collective-permute-start.3 = (bf16[128,2048]{0,1:T(8,128)(2,1)}, bf16[128,2048]{0,1:T(8,128)(2,1)}, u32[]{:S(2)}, u32[]{:S(2)}) collective-permute-start(bf16[128,2048]{0,1:T(8,128)(2,1)} %collective-permute-done.1), channel_id=1, source_target_pairs={{0,28},{4,0},{8,4},{12,8},{16,12},{20,16},{24,20},{28,24},{1,29},{... | collective-permute-start | bytes 1572872 | tf_op jit(solution)/shard_map/ppermute | solution.py:28
  145.7 14.9 %collective-permute-start.4 = (bf16[128,2048]{0,1:T(8,128)(2,1)}, bf16[128,2048]{0,1:T(8,128)(2,1)S(1)}, u32[]{:S(2)}, u32[]{:S(2)}) collective-permute-start(bf16[128,2048]{0,1:T(8,128)(2,1)} %collective-permute-done.2), channel_id=1, source_target_pairs={{0,4},{4,8},{8,12},{12,16},{16,20},{20,24},{24,28},{28,0},{1,5},{5... | collective-permute-start | bytes 1572872 | tf_op jit(solution)/shard_map/ppermute | solution.py:25
  155.9 21.6 %collective-permute-start.5 = (bf16[128,2048]{0,1:T(8,128)(2,1)}, bf16[128,2048]{0,1:T(8,128)(2,1)S(1)}, u32[]{:S(2)}, u32[]{:S(2)}) collective-permute-start(bf16[128,2048]{0,1:T(8,128)(2,1)} %collective-permute-done.3), channel_id=1, source_target_pairs={{0,28},{4,0},{8,4},{12,8},{16,12},{20,16},{24,20},{28,24},{1,29},{... | collective-permute-start | bytes 1572872 | tf_op jit(solution)/shard_map/ppermute | solution.py:28
  160.6 18.9 %collective-permute-start.6 = (bf16[128,2048]{0,1:T(8,128)(2,1)S(1)}, bf16[128,2048]{0,1:T(8,128)(2,1)S(1)}, u32[]{:S(2)}, u32[]{:S(2)}) collective-permute-start(bf16[128,2048]{0,1:T(8,128)(2,1)S(1)} %collective-permute-done.4), channel_id=1, source_target_pairs={{0,4},{4,8},{8,12},{12,16},{16,20},{20,24},{24,28},{28,0},{1,5},{5... | collective-permute-start | bytes 1572872 | tf_op jit(solution)/shard_map/ppermute | solution.py:25
  259.5 55.5 %reduce-scatter.14.cloned.1.call-start = ((), (), s32[]{:S(2)}) async-start(), calls=%async_computation.12 | async-start | bytes 1310720 | tf_op jit(solution)/shard_map/reduce_scatter | solution.py:224
  265.9 78.3 %all-gather.17.cloned.1.call-start = ((), (), s32[]{:S(2)}) async-start(), calls=%async_computation.15 | async-start | bytes 1310720 | tf_op jit(solution)/shard_map/all_gather | solution.py:237
  317.5 63.8 %reduce-scatter.18.cloned.1.call-start = ((), (), s32[]{:S(2)}) async-start(), calls=%async_computation.16 | async-start | bytes 1310720 | tf_op jit(solution)/shard_map/reduce_scatter | solution.py:265
  353.8 71.8 %reduce-scatter.22.cloned.1.call-start = ((), (), s32[]{:S(2)}) async-start(), calls=%async_computation.18 | async-start | bytes 1769472
  358.1 118.2 %reduce-scatter.24.cloned.1.call-start = ((), (), s32[]{:S(2)}) async-start(), calls=%async_computation.19 | async-start | bytes 4718592
  370.9 180.4 %reduce-scatter.20.cloned.1.call-start = ((), (), s32[]{:S(2)}) async-start(), calls=%async_computation.17 | async-start | bytes 9437184 | tf_op jit(solution)/shard_map/reduce_scatter | solution.py:229
  381.1 41.9 %copy-start.37 = (f32[2,128]{1,0:T(2,128)S(1)}, f32[2,128]{1,0:T(2,128)}, u32[]{:S(2)}) copy-start(f32[2,128]{1,0:T(2,128)} %param.28) | copy-start | bytes 3076
  381.1 42.5 %copy-start.12 = (f32[128,1024]{1,0:T(8,128)S(1)}, f32[128,1024]{1,0:T(8,128)}, u32[]{:S(2)}) copy-start(f32[128,1024]{1,0:T(8,128)} %get-tuple-element.94) | copy-start | bytes 1572868
  381.1 42.4 %copy-start.39 = (f32[128]{0:T(128)S(1)}, f32[128]{0:T(128)}, u32[]{:S(2)}) copy-start(f32[128]{0:T(128)} %get-tuple-element.113) | copy-start | bytes 1540
  381.2 45.7 %copy-start.21 = (f32[2,128,128]{2,1,0:T(8,128)S(1)}, f32[2,128,128]{2,1,0:T(8,128)}, u32[]{:S(2)}) copy-start(f32[2,128,128]{2,1,0:T(8,128)} %param.25) | copy-start | bytes 393220
  381.2 45.7 %copy-start.28 = (f32[2,128,128]{2,1,0:T(8,128)S(1)}, f32[2,128,128]{2,1,0:T(8,128)}, u32[]{:S(2)}) copy-start(f32[2,128,128]{2,1,0:T(8,128)} %param.32) | copy-start | bytes 393220
  381.2 45.7 %copy-start.29 = (f32[2,128,128]{2,1,0:T(8,128)S(1)}, f32[2,128,128]{2,1,0:T(8,128)}, u32[]{:S(2)}) copy-start(f32[2,128,128]{2,1,0:T(8,128)} %param.33) | copy-start | bytes 393220
  381.2 46.5 %copy-start.15 = (f32[4,128,128]{2,1,0:T(8,128)S(1)}, f32[4,128,128]{2,1,0:T(8,128)}, u32[]{:S(2)}) copy-start(f32[4,128,128]{2,1,0:T(8,128)} %param.24) | copy-start | bytes 786436
  381.2 46.5 %copy-start.26 = (f32[4,128,128]{2,1,0:T(8,128)S(1)}, f32[4,128,128]{2,1,0:T(8,128)}, u32[]{:S(2)}) copy-start(f32[4,128,128]{2,1,0:T(8,128)} %param.30) | copy-start | bytes 786436
  381.2 46.5 %copy-start.27 = (f32[4,128,128]{2,1,0:T(8,128)S(1)}, f32[4,128,128]{2,1,0:T(8,128)}, u32[]{:S(2)}) copy-start(f32[4,128,128]{2,1,0:T(8,128)} %param.31) | copy-start | bytes 786436
  423.6 54.2 %copy-start.4 = (f32[16,128,128]{2,1,0:T(8,128)S(1)}, f32[16,128,128]{2,1,0:T(8,128)}, u32[]{:S(2)}) copy-start(f32[16,128,128]{2,1,0:T(8,128)} %param.27) | copy-start | bytes 3145732
  477.8 75.0 %copy-start.6 = (f32[128,16,128]{2,0,1:T(8,128)}, f32[128,16,128]{2,0,1:T(8,128)S(1)}, u32[]{:S(2)}) copy-start(f32[128,16,128]{2,0,1:T(8,128)S(1)} %copy.102) | copy-start | bytes 3145732
  (35 other events, 256.1 us)
Sparse Core Ops, SparseCore 0:
  21.9 28.2 all-gather.6
  52.7 25.1 all-gather.8
  86.6 27.2 reduce-scatter.11
  117.0 26.4 all-gather.10
  145.8 62.5 all-gather.12
  210.4 27.9 all-gather.14
  259.6 26.6 reduce-scatter.15
  289.2 25.7 reduce-scatter.13
  317.6 26.4 all-gather.16
  354.0 26.6 reduce-scatter.17
  384.5 37.0 reduce-scatter.21
  424.9 51.3 reduce-scatter.23
  479.7 71.4 reduce-scatter.19
